TPU v7x, 32 devices: a whole 2x2x4 slice. The times are simulated.
32 devices in a mesh: band: 4 (over z), roster: 8 (over y, x, core).
Axes of the slice: x: 2, y: 2, z: 4, core: 2. Of those that a mesh axis runs over, the one named last changes fastest.
Arguments:
- tiles: bfloat16 [4, 8, 6, 256, 256], P('band', 'roster'), as said below
- tile_slots: int32 [4, 8, 6], P('band', 'roster'), may hold values from 0 to 5, each once within a row
- tile_count: int32 [4, 8], P('band', 'roster'), may hold values from 1 to 6, as said below
- costs: float32 [6144, 128], P('roster'), may hold values from 1000 to 10000
- primal_start: float32 [6144, 128], P('roster'), may hold values from 0 to 1
- dual_start: float32 [2048, 128], P('band'), may hold values from 0.5 to 4
Outputs:
- primal: float32 [6144, 128], P('roster')
- dual: float32 [2048, 128], P('band')
Inputs may be any that keep to these rules, and one draw needn't show every extreme that they name: `tile_slots`: each device's slots list every tile position once; slot s is in use where s < tile_count. `tile_count`: some device uses all 6 slots. `tiles`: entries are zero or positive.
All inputs are finite; a program needn't handle non-finite values.
Results may differ from a plain program's by a relative error of at most 0.0003.
Values sent between devices are 32-bit elements; how exact they have to be, the bound alone decides.
A program may use at most 64 MiB of HBM per device.

v0:
```python
import jax
import jax.numpy as jnp
from jax import lax
from jax.sharding import PartitionSpec as P

ROUNDS = 3
ITERS = 4
HIGH = lax.Precision.HIGHEST
eps = 1e-06


def shards(tiles, tile_slots, tile_count, costs, primal_start, dual_start):
    tile_block = tiles[0, 0]
    slots = tile_slots[0, 0]
    count = tile_count[0, 0]
    tile = tile_block.shape[1]
    rows = dual_start.shape[0]
    cols = costs.shape[0]
    row_tiles = rows // tile
    col_tiles = cols // tile
    row_index = slots // col_tiles
    col_index = slots % col_tiles
    active = (jnp.arange(slots.shape[0], dtype=jnp.int32) < count).astype(jnp.float32)
    row_hot = (row_index[None, :] == jnp.arange(row_tiles, dtype=jnp.int32)[:, None]).astype(
        jnp.float32
    )
    col_hot = (col_index[None, :] == jnp.arange(col_tiles, dtype=jnp.int32)[:, None]).astype(
        jnp.float32
    )

    def scale_tiles(row_scale, col_scale):
        row_part = row_scale.reshape(row_tiles, tile)[row_index]
        col_part = col_scale.reshape(col_tiles, tile)[col_index]
        return (
            tile_block.astype(jnp.float32)
            * row_part[:, :, None]
            * col_part[:, None, :]
            * active[:, None, None]
        )

    row_scale = jnp.ones((rows,), jnp.float32)
    col_scale = jnp.ones((cols,), jnp.float32)
    for turn in range(ROUNDS):
        magnitude = jnp.abs(scale_tiles(row_scale, col_scale))
        slot_rows = jnp.max(magnitude, axis=2)
        slot_cols = jnp.max(magnitude, axis=1)
        row_peak = jnp.max(row_hot[:, :, None] * slot_rows[None], axis=1).reshape(-1)
        col_peak = jnp.max(col_hot[:, :, None] * slot_cols[None], axis=1).reshape(-1)
        row_peak = lax.pmax(row_peak, "roster")
        col_peak = lax.pmax(col_peak, "band")
        row_scale = row_scale / jnp.sqrt(row_peak + eps)
        col_scale = col_scale / jnp.sqrt(col_peak + eps)
    scaled = scale_tiles(row_scale, col_scale)
    squares = lax.psum(jnp.sum(scaled * scaled), ("band", "roster"))
    eta = 0.9 / jnp.sqrt(squares + eps)
    scen = costs.shape[1]
    col_full = col_scale[:, None]
    row_full = row_scale[:, None]
    cost_t = costs * col_full
    upper = 1.0 / col_full
    primal = primal_start / col_full
    dual = dual_start / row_full
    for step in range(ITERS):
        dual_slots = dual.reshape(row_tiles, tile, scen)[row_index]
        back_terms = jnp.einsum("sij,sik->sjk", scaled, dual_slots, precision=HIGH)
        g_local = jnp.einsum("cs,sjk->cjk", col_hot, back_terms, precision=HIGH).reshape(cols, scen)
        g_whole = lax.psum(g_local, "band")
        primal_next = jnp.clip(primal - eta * (cost_t - g_whole), 0.0, upper)
        extrapolated = 2.0 * primal_next - primal
        primal_slots = extrapolated.reshape(col_tiles, tile, scen)[col_index]
        fore_terms = jnp.einsum("sij,sjk->sik", scaled, primal_slots, precision=HIGH)
        h_local = jnp.einsum("rs,sik->rik", row_hot, fore_terms, precision=HIGH).reshape(rows, scen)
        share = rows // lax.axis_size("roster")
        begin = lax.axis_index("roster") * share
        h_share = lax.psum_scatter(h_local, "roster", scatter_dimension=0, tiled=True)
        own_dual = lax.dynamic_slice_in_dim(dual, begin, share, 0)
        own_rows = lax.dynamic_slice_in_dim(row_full, begin, share, 0)
        dual_share = own_dual + eta * (own_rows - h_share)
        dual = lax.all_gather(dual_share, "roster", axis=0, tiled=True)
        primal = primal_next
    return (primal, dual)


def solution(mesh):
    placed = (
        P("band", "roster", None, None, None),
        P("band", "roster", None),
        P("band", "roster"),
        P("roster", None),
        P("roster", None),
        P("band", None),
    )
    return jax.shard_map(
        shards,
        mesh=mesh,
        in_specs=placed,
        out_specs=(P("roster", None), P("band", None)),
        check_vma=False,
    )
```

profile of v0, /device:TPU:0, one launch (start us, length us, event | category | flops | bytes accessed | tf_op | source)
XLA Modules:
  0.0 466.0 jit_solution(17935510203944272796)
XLA Ops:
  10.5 1.8 fusion.3
  12.4 15.1 %pmax.43 = f32[512]{0:T(512)S(1)} all-reduce(f32[512]{0:T(512)S(1)} %bitcast.135), channel_id=1, replica_groups=mesh['band'=4,'roster'=8] {'roster'}, use_global_device_ids=true, to_apply=%region_5.6 | all-reduce | flops 512 | bytes 4096 | tf_op jit(solution)/shard_map/pmax | solution.py:49
  27.7 12.0 %pmax.42 = f32[768]{0:T(1024)S(1)} all-reduce(f32[768]{0:T(1024)S(1)} %reshape.279), channel_id=1, replica_groups=mesh['band'=4,'roster'=8] {'band'}, use_global_device_ids=true, to_apply=%region_2.3 | all-reduce | flops 768 | bytes 6144 | tf_op jit(solution)/shard_map/pmax | solution.py:50
  41.6 8.4 %pmax.44 = f32[768]{0:T(1024)S(1)} all-reduce(f32[768]{0:T(1024)S(1)} %reshape.283), channel_id=1, replica_groups=mesh['band'=4,'roster'=8] {'band'}, use_global_device_ids=true, to_apply=%region_8.9 | all-reduce | flops 768 | bytes 6144 | tf_op jit(solution)/shard_map/pmax | solution.py:50
  50.0 11.8 %pmax.45 = f32[512]{0:T(512)S(1)} all-reduce(f32[512]{0:T(512)S(1)} %bitcast.136), channel_id=1, replica_groups=mesh['band'=4,'roster'=8] {'roster'}, use_global_device_ids=true, to_apply=%region_11.12 | all-reduce | flops 512 | bytes 4096 | tf_op jit(solution)/shard_map/pmax | solution.py:49
  63.8 10.4 %pmax.46 = f32[768]{0:T(1024)S(1)} all-reduce(f32[768]{0:T(1024)S(1)} %reshape.287), channel_id=1, replica_groups=mesh['band'=4,'roster'=8] {'band'}, use_global_device_ids=true, to_apply=%region_14.15 | all-reduce | flops 768 | bytes 6144 | tf_op jit(solution)/shard_map/pmax | solution.py:50
  74.2 11.8 %pmax.47 = f32[512]{0:T(512)S(1)} all-reduce(f32[512]{0:T(512)S(1)} %bitcast.137), channel_id=1, replica_groups=mesh['band'=4,'roster'=8] {'roster'}, use_global_device_ids=true, to_apply=%region_17.18 | all-reduce | flops 512 | bytes 4096 | tf_op jit(solution)/shard_map/pmax | solution.py:49
  87.9 2.9 fusion.31
  92.8 1.2 fusion.34
  93.9 37.9 %psum.35 = f32[]{:T(128)} all-reduce(f32[]{:T(128)} %fusion.34), channel_id=1, replica_groups=mesh['band'=4,'roster'=8] {'band','roster'}, use_global_device_ids=true, to_apply=%region_19.20 | all-reduce | flops 1 | bytes 8 | tf_op jit(solution)/shard_map/psum | solution.py:54
  132.6 1.3 multiply_subtract_fusion.3
  134.5 1.8 fusion.29
  138.2 33.9 %reduce-scatter.5.cloned.1.call-done = f32[64,128]{1,0:T(8,128)} async-done(((f32[512,128]{1,0:T(8,128)}), f32[64,128]{1,0:T(8,128)}) %reduce-scatter.5.cloned.1.call-update) | async-done | bytes 32784 | tf_op jit(solution)/shard_map/reduce_scatter | solution.py:75
  172.8 9.7 %all_gather.12 = f32[512,128]{1,0:T(8,128)S(1)} all-gather(f32[64,128]{1,0:T(8,128)S(1)} %multiply_add_fusion.3), channel_id=1, replica_groups=mesh['band'=4,'roster'=8] {'roster'}, dimensions={0}, use_global_device_ids=true | all-gather | bytes 294912 | tf_op jit(solution)/shard_map/all_gather | solution.py:79
  183.2 3.0 fusion.27
  188.0 37.0 %all-reduce.7.cloned.1.call-done = f32[768,128]{1,0:T(8,128)} async-done(((f32[768,128]{1,0:T(8,128)}), f32[768,128]{1,0:T(8,128)}) %all-reduce.7.cloned.1.call-update) | async-done | bytes 393232 | tf_op jit(solution)/shard_map/psum | solution.py:67
  225.0 1.3 multiply_subtract_fusion.2
  226.9 1.8 fusion.25
  230.4 33.5 %reduce-scatter.7.cloned.1.call-done = f32[64,128]{1,0:T(8,128)} async-done(((f32[512,128]{1,0:T(8,128)}), f32[64,128]{1,0:T(8,128)}) %reduce-scatter.7.cloned.1.call-update) | async-done | bytes 32784 | tf_op jit(solution)/shard_map/reduce_scatter | solution.py:75
  264.8 9.4 %all_gather.13 = f32[512,128]{1,0:T(8,128)S(1)} all-gather(f32[64,128]{1,0:T(8,128)S(1)} %multiply_add_fusion.2), channel_id=1, replica_groups=mesh['band'=4,'roster'=8] {'roster'}, dimensions={0}, use_global_device_ids=true | all-gather | bytes 294912 | tf_op jit(solution)/shard_map/all_gather | solution.py:79
  274.8 3.0 fusion.23
  279.6 37.1 %all-reduce.9.cloned.1.call-done = f32[768,128]{1,0:T(8,128)} async-done(((f32[768,128]{1,0:T(8,128)}), f32[768,128]{1,0:T(8,128)}) %all-reduce.9.cloned.1.call-update) | async-done | bytes 393232 | tf_op jit(solution)/shard_map/psum | solution.py:67
  316.7 1.3 multiply_subtract_fusion.1
  318.6 1.8 fusion.21
  322.1 33.5 %reduce-scatter.9.cloned.1.call-done = f32[64,128]{1,0:T(8,128)} async-done(((f32[512,128]{1,0:T(8,128)}), f32[64,128]{1,0:T(8,128)}) %reduce-scatter.9.cloned.1.call-update) | async-done | bytes 32784 | tf_op jit(solution)/shard_map/reduce_scatter | solution.py:75
  356.5 9.5 %all_gather.14 = f32[512,128]{1,0:T(8,128)S(1)} all-gather(f32[64,128]{1,0:T(8,128)S(1)} %multiply_add_fusion.1), channel_id=1, replica_groups=mesh['band'=4,'roster'=8] {'roster'}, dimensions={0}, use_global_device_ids=true | all-gather | bytes 294912 | tf_op jit(solution)/shard_map/all_gather | solution.py:79
  366.6 3.0 fusion.19
  371.4 37.1 %all-reduce.11.cloned.1.call-done = f32[768,128]{1,0:T(8,128)} async-done(((f32[768,128]{1,0:T(8,128)}), f32[768,128]{1,0:T(8,128)}) %all-reduce.11.cloned.1.call-update) | async-done | bytes 393232 | tf_op jit(solution)/shard_map/psum | solution.py:67
  408.4 2.0 multiply_subtract_fusion
  411.1 1.8 fusion.17
  414.6 33.6 %reduce-scatter.11.cloned.1.call-done = f32[64,128]{1,0:T(8,128)} async-done(((f32[512,128]{1,0:T(8,128)}), f32[64,128]{1,0:T(8,128)}) %reduce-scatter.11.cloned.1.call-update) | async-done | bytes 32784 | tf_op jit(solution)/shard_map/reduce_scatter | solution.py:75
  449.0 9.2 %all_gather.15 = f32[512,128]{1,0:T(8,128)S(1)} all-gather(f32[64,128]{1,0:T(8,128)S(1)} %multiply_add_fusion), channel_id=1, replica_groups=mesh['band'=4,'roster'=8] {'roster'}, dimensions={0}, use_global_device_ids=true | all-gather | bytes 294912 | tf_op jit(solution)/shard_map/all_gather | solution.py:79
  (99 shorter events, 31.4 us)
Async XLA Ops:
  7.2 33.6 %copy-start = (bf16[1,1,6,256,256]{4,3,2,1,0:T(8,128)(2,1)S(1)}, bf16[1,1,6,256,256]{4,3,2,1,0:T(8,128)(2,1)}, u32[]{:S(2)}) copy-start(bf16[1,1,6,256,256]{4,3,2,1,0:T(8,128)(2,1)} %param.6) | copy-start | bytes 2359300
  7.2 125.4 %all-reduce.5.cloned.1.call-start = ((), (), s32[]{:S(2)}) async-start(), calls=%async_computation.4 | async-start | bytes 786432 | tf_op jit(solution)/shard_map/psum | solution.py:67
  41.4 45.7 %copy-start.3 = (f32[512,128]{1,0:T(8,128)S(1)}, f32[512,128]{1,0:T(8,128)}, u32[]{:S(2)}) copy-start(f32[512,128]{1,0:T(8,128)} %param.11) | copy-start | bytes 786436
  92.7 39.9 %copy-start.1 = (f32[768,128]{1,0:T(8,128)S(1)}, f32[768,128]{1,0:T(8,128)}, u32[]{:S(2)}) copy-start(f32[768,128]{1,0:T(8,128)} %param.9) | copy-start | bytes 1179652
  92.7 39.9 %copy-start.2 = (f32[768,128]{1,0:T(8,128)S(1)}, f32[768,128]{1,0:T(8,128)}, u32[]{:S(2)}) copy-start(f32[768,128]{1,0:T(8,128)} %param.10) | copy-start | bytes 1179652
  92.7 79.3 %reduce-scatter.5.cloned.1.call-start = ((), (), s32[]{:S(2)}) async-start(), calls=%async_computation.5 | async-start | bytes 294912 | tf_op jit(solution)/shard_map/reduce_scatter | solution.py:75
  138.0 87.0 %all-reduce.7.cloned.1.call-start = ((), (), s32[]{:S(2)}) async-start(), calls=%async_computation.6 | async-start | bytes 786432 | tf_op jit(solution)/shard_map/psum | solution.py:67
  187.9 76.1 %reduce-scatter.7.cloned.1.call-start = ((), (), s32[]{:S(2)}) async-start(), calls=%async_computation.7 | async-start | bytes 294912 | tf_op jit(solution)/shard_map/reduce_scatter | solution.py:75
  230.4 86.3 %all-reduce.9.cloned.1.call-start = ((), (), s32[]{:S(2)}) async-start(), calls=%async_computation.8 | async-start | bytes 786432 | tf_op jit(solution)/shard_map/psum | solution.py:67
  279.6 76.1 %reduce-scatter.9.cloned.1.call-start = ((), (), s32[]{:S(2)}) async-start(), calls=%async_computation.9 | async-start | bytes 294912 | tf_op jit(solution)/shard_map/reduce_scatter | solution.py:75
  322.1 86.4 %all-reduce.11.cloned.1.call-start = ((), (), s32[]{:S(2)}) async-start(), calls=%async_computation.10 | async-start | bytes 786432 | tf_op jit(solution)/shard_map/psum | solution.py:67
  371.3 76.8 %reduce-scatter.11.cloned.1.call-start = ((), (), s32[]{:S(2)}) async-start(), calls=%async_computation.11 | async-start | bytes 294912 | tf_op jit(solution)/shard_map/reduce_scatter | solution.py:75
Sparse Core Ops, SparseCore 0:
  92.8 33.2 all-reduce.4
  138.1 33.8 reduce-scatter.4
  188.0 36.9 all-reduce.6
  230.5 33.4 reduce-scatter.6
  279.7 36.9 all-reduce.8
  322.2 33.4 reduce-scatter.8
  371.5 36.9 all-reduce.10
  414.7 33.4 reduce-scatter.10
where the time goes:
time: 475 us; the launch traced here: 466 us
  waiting for transfers between devices  246 us (52%)
  blocking collectives  145 us (31%)
  matrix products  26.8 us (6%)
  local copies, waits for them, and re-layouts  16.3 us (3%)
  between operations  16.1 us (3%)
  other arithmetic  15.4 us (3%)
    reduce_scatter x4, waiting for transfers between devices, shards(): lax.psum_scatter(h_local, 'roster', scatter_dimension=0, tiled=True)  135 us
    psum x4, waiting for transfers between devices, shards(): g_whole = lax.psum(g_local, 'band')  111 us
    pmax x3, blocking collectives, shards(): row_peak = lax.pmax(row_peak, 'roster')  38.7 us
    psum x1, blocking collectives, shards(): squares = lax.psum(jnp.sum(scaled * scaled), ('band', 'roster'))  37.9 us
    all_gather x4, blocking collectives, shards(): dual = lax.all_gather(dual_share, 'roster', axis=0, tiled=True)  37.8 us
    pmax x3, blocking collectives, shards(): col_peak = lax.pmax(col_peak, 'band')  30.7 us
    dot_general x4, matrix products, shards(): back_terms = jnp.einsum('sij,sik->sjk', scaled, dual_slots, precision=HIGH)  11.8 us
  transfers between devices with their start and end apart: 8, of which 7 were waited for; matrix products, arithmetic and copies ran while one was open for 0% of the time, Pallas kernels for 0%

commit v1 on v0

--- a/solution.py
+++ b/solution.py
@@ -7,6 +7,16 @@
 ITERS = 4
 HIGH = lax.Precision.HIGHEST
 eps = 1e-06
+
+
+def turned_line(value, mesh_axis, dim):
+    size = lax.axis_size(mesh_axis)
+    block, blocks = (value, [value])
+    for _ in range(size - 1):
+        block = lax.ppermute(block, mesh_axis, [(i, (i + 1) % size) for i in range(size)])
+        blocks.insert(0, block)
+    line = jnp.concatenate(blocks, axis=dim)
+    return jnp.roll(line, (lax.axis_index(mesh_axis) + 1) * value.shape[dim], axis=dim)
 
 
 def shards(tiles, tile_slots, tile_count, costs, primal_start, dual_start):
@@ -76,7 +86,7 @@
         own_dual = lax.dynamic_slice_in_dim(dual, begin, share, 0)
         own_rows = lax.dynamic_slice_in_dim(row_full, begin, share, 0)
         dual_share = own_dual + eta * (own_rows - h_share)
-        dual = lax.all_gather(dual_share, "roster", axis=0, tiled=True)
+        dual = turned_line(dual_share, "roster", 0)
         primal = primal_next
     return (primal, dual)
 

time: 475 us -> 558 us (1.17)
  waiting for transfers between devices: 246 us -> 364 us
  blocking collectives: 145 us -> 107 us
    ppermute x0 -> x28, waiting for transfers between devices: none -> 119 us  [turned_line(): lax.ppermute(block, mesh_axis, [(i, (i + 1) % size) for i in range(size)])]
    all_gather x4 -> x0, blocking collectives: 37.8 us -> none  [shards(): dual = lax.all_gather(dual_share, 'roster', axis=0, tiled=True)]
  transfers between devices with their start and end apart: 8 -> 36, of which waited for: 7 -> 35; matrix products, arithmetic and copies ran while one was open for 0% -> 0% of each run, Pallas kernels for 0% -> 0%
where the time goes in v1:
time: 558 us; the launch traced here: 549 us
  waiting for transfers between devices  364 us (65%)
  blocking collectives  107 us (19%)
  matrix products  26.8 us (5%)
  other arithmetic  16.8 us (3%)
  between operations  16.4 us (3%)
  local copies, waits for them, and re-layouts  15.7 us (3%)
    reduce_scatter x4, waiting for transfers between devices, shards(): lax.psum_scatter(h_local, 'roster', scatter_dimension=0, tiled=True)  134 us
    ppermute x28, waiting for transfers between devices, turned_line(): lax.ppermute(block, mesh_axis, [(i, (i + 1) % size) for i in range(size)])  119 us
    psum x4, waiting for transfers between devices, shards(): g_whole = lax.psum(g_local, 'band')  111 us
    pmax x3, blocking collectives, shards(): row_peak = lax.pmax(row_peak, 'roster')  38.7 us
    psum x1, blocking collectives, shards(): squares = lax.psum(jnp.sum(scaled * scaled), ('band', 'roster'))  38 us
    pmax x3, blocking collectives, shards(): col_peak = lax.pmax(col_peak, 'band')  30.7 us
    dot_general x4, matrix products, shards(): back_terms = jnp.einsum('sij,sik->sjk', scaled, dual_slots, precision=HIGH)  11.8 us
  transfers between devices with their start and end apart: 36, of which 35 were waited for; matrix products, arithmetic and copies ran while one was open for 0% of the time, Pallas kernels for 0%

profile of v1, /device:TPU:0, one launch (start us, length us, event | category | flops | bytes accessed | tf_op | source)
XLA Modules:
  0.0 548.8 jit_solution(10455361344656175418)
XLA Ops:
  12.4 15.1 %pmax.43 = f32[512]{0:T(512)S(1)} all-reduce(f32[512]{0:T(512)S(1)} %bitcast.135), channel_id=1, replica_groups=mesh['band'=4,'roster'=8] {'roster'}, use_global_device_ids=true, to_apply=%region_5.6 | all-reduce | flops 512 | bytes 4096 | tf_op jit(solution)/shard_map/pmax | solution.py:59
  27.7 12.0 %pmax.42 = f32[768]{0:T(1024)S(1)} all-reduce(f32[768]{0:T(1024)S(1)} %reshape.279), channel_id=1, replica_groups=mesh['band'=4,'roster'=8] {'band'}, use_global_device_ids=true, to_apply=%region_2.3 | all-reduce | flops 768 | bytes 6144 | tf_op jit(solution)/shard_map/pmax | solution.py:60
  41.6 8.4 %pmax.44 = f32[768]{0:T(1024)S(1)} all-reduce(f32[768]{0:T(1024)S(1)} %reshape.283), channel_id=1, replica_groups=mesh['band'=4,'roster'=8] {'band'}, use_global_device_ids=true, to_apply=%region_8.9 | all-reduce | flops 768 | bytes 6144 | tf_op jit(solution)/shard_map/pmax | solution.py:60
  50.0 11.8 %pmax.45 = f32[512]{0:T(512)S(1)} all-reduce(f32[512]{0:T(512)S(1)} %bitcast.136), channel_id=1, replica_groups=mesh['band'=4,'roster'=8] {'roster'}, use_global_device_ids=true, to_apply=%region_11.12 | all-reduce | flops 512 | bytes 4096 | tf_op jit(solution)/shard_map/pmax | solution.py:59
  63.8 10.4 %pmax.46 = f32[768]{0:T(1024)S(1)} all-reduce(f32[768]{0:T(1024)S(1)} %reshape.287), channel_id=1, replica_groups=mesh['band'=4,'roster'=8] {'band'}, use_global_device_ids=true, to_apply=%region_14.15 | all-reduce | flops 768 | bytes 6144 | tf_op jit(solution)/shard_map/pmax | solution.py:60
  74.2 11.8 %pmax.47 = f32[512]{0:T(512)S(1)} all-reduce(f32[512]{0:T(512)S(1)} %bitcast.137), channel_id=1, replica_groups=mesh['band'=4,'roster'=8] {'roster'}, use_global_device_ids=true, to_apply=%region_17.18 | all-reduce | flops 512 | bytes 4096 | tf_op jit(solution)/shard_map/pmax | solution.py:59
  93.9 38.0 %psum.35 = f32[]{:T(128)} all-reduce(f32[]{:T(128)} %fusion.34), channel_id=1, replica_groups=mesh['band'=4,'roster'=8] {'band','roster'}, use_global_device_ids=true, to_apply=%region_19.20 | all-reduce | flops 1 | bytes 8 | tf_op jit(solution)/shard_map/psum | solution.py:64
  138.2 33.8 %reduce-scatter.5.cloned.1.call-done = f32[64,128]{1,0:T(8,128)} async-done(((f32[512,128]{1,0:T(8,128)}), f32[64,128]{1,0:T(8,128)}) %reduce-scatter.5.cloned.1.call-update) | async-done | bytes 32784 | tf_op jit(solution)/shard_map/reduce_scatter | solution.py:85
  177.5 4.2 collective-permute-done.1
  181.8 4.2 collective-permute-done.2
  186.0 4.2 collective-permute-done.3
  190.3 4.2 collective-permute-done.4
  194.5 4.2 collective-permute-done.5
  198.7 4.2 collective-permute-done.6
  208.6 37.1 %all-reduce.7.cloned.1.call-done = f32[768,128]{1,0:T(8,128)} async-done(((f32[768,128]{1,0:T(8,128)}), f32[768,128]{1,0:T(8,128)}) %all-reduce.7.cloned.1.call-update) | async-done | bytes 393232 | tf_op jit(solution)/shard_map/psum | solution.py:77
  251.2 33.5 %reduce-scatter.7.cloned.1.call-done = f32[64,128]{1,0:T(8,128)} async-done(((f32[512,128]{1,0:T(8,128)}), f32[64,128]{1,0:T(8,128)}) %reduce-scatter.7.cloned.1.call-update) | async-done | bytes 32784 | tf_op jit(solution)/shard_map/reduce_scatter | solution.py:85
  289.8 4.2 collective-permute-done.8
  294.0 4.2 collective-permute-done.9
  298.3 4.2 collective-permute-done.10
  302.5 4.2 collective-permute-done.11
  306.8 4.2 collective-permute-done.12
  321.1 37.0 %all-reduce.9.cloned.1.call-done = f32[768,128]{1,0:T(8,128)} async-done(((f32[768,128]{1,0:T(8,128)}), f32[768,128]{1,0:T(8,128)}) %all-reduce.9.cloned.1.call-update) | async-done | bytes 393232 | tf_op jit(solution)/shard_map/psum | solution.py:77
  363.6 33.5 %reduce-scatter.9.cloned.1.call-done = f32[64,128]{1,0:T(8,128)} async-done(((f32[512,128]{1,0:T(8,128)}), f32[64,128]{1,0:T(8,128)}) %reduce-scatter.9.cloned.1.call-update) | async-done | bytes 32784 | tf_op jit(solution)/shard_map/reduce_scatter | solution.py:85
  402.2 4.2 collective-permute-done.15
  406.4 4.2 collective-permute-done.16
  410.7 4.2 collective-permute-done.17
  414.9 4.2 collective-permute-done.18
  419.1 4.2 collective-permute-done.19
  433.5 37.0 %all-reduce.11.cloned.1.call-done = f32[768,128]{1,0:T(8,128)} async-done(((f32[768,128]{1,0:T(8,128)}), f32[768,128]{1,0:T(8,128)}) %all-reduce.11.cloned.1.call-update) | async-done | bytes 393232 | tf_op jit(solution)/shard_map/psum | solution.py:77
  476.7 33.6 %reduce-scatter.11.cloned.1.call-done = f32[64,128]{1,0:T(8,128)} async-done(((f32[512,128]{1,0:T(8,128)}), f32[64,128]{1,0:T(8,128)}) %reduce-scatter.11.cloned.1.call-update) | async-done | bytes 32784 | tf_op jit(solution)/shard_map/reduce_scatter | solution.py:85
  515.4 4.2 collective-permute-done.22
  528.1 4.2 collective-permute-done.25
  (186 shorter events, 103.1 us)
Async XLA Ops:
  7.2 125.4 %all-reduce.5.cloned.1.call-start = ((), (), s32[]{:S(2)}) async-start(), calls=%async_computation.4 | async-start | bytes 786432 | tf_op jit(solution)/shard_map/psum | solution.py:77
  92.7 79.3 %reduce-scatter.5.cloned.1.call-start = ((), (), s32[]{:S(2)}) async-start(), calls=%async_computation.5 | async-start | bytes 294912 | tf_op jit(solution)/shard_map/reduce_scatter | solution.py:85
  138.0 107.7 %all-reduce.7.cloned.1.call-start = ((), (), s32[]{:S(2)}) async-start(), calls=%async_computation.6 | async-start | bytes 786432 | tf_op jit(solution)/shard_map/psum | solution.py:77
  172.8 4.7 collective-permute-start
  177.5 4.2 collective-permute-start.1
  181.8 4.2 collective-permute-start.2
  186.0 4.2 collective-permute-start.3
  190.3 4.2 collective-permute-start.4
  194.5 4.2 collective-permute-start.5
  198.7 4.2 collective-permute-start.6
  208.6 76.1 %reduce-scatter.7.cloned.1.call-start = ((), (), s32[]{:S(2)}) async-start(), calls=%async_computation.7 | async-start | bytes 294912 | tf_op jit(solution)/shard_map/reduce_scatter | solution.py:85
  251.1 107.0 %all-reduce.9.cloned.1.call-start = ((), (), s32[]{:S(2)}) async-start(), calls=%async_computation.8 | async-start | bytes 786432 | tf_op jit(solution)/shard_map/psum | solution.py:77
  285.5 4.3 collective-permute-start.7
  289.8 4.2 collective-permute-start.8
  294.0 4.2 collective-permute-start.9
  298.3 4.2 collective-permute-start.10
  302.5 4.2 collective-permute-start.11
  306.8 4.2 collective-permute-start.12
  311.0 4.4 collective-permute-start.13
  321.0 76.1 %reduce-scatter.9.cloned.1.call-start = ((), (), s32[]{:S(2)}) async-start(), calls=%async_computation.9 | async-start | bytes 294912 | tf_op jit(solution)/shard_map/reduce_scatter | solution.py:85
  363.5 107.0 %all-reduce.11.cloned.1.call-start = ((), (), s32[]{:S(2)}) async-start(), calls=%async_computation.10 | async-start | bytes 786432 | tf_op jit(solution)/shard_map/psum | solution.py:77
  397.9 4.3 collective-permute-start.14
  402.2 4.2 collective-permute-start.15
  406.4 4.2 collective-permute-start.16
  410.7 4.2 collective-permute-start.17
  414.9 4.2 collective-permute-start.18
  419.1 4.2 collective-permute-start.19
  423.4 4.4 collective-permute-start.20
  433.4 76.8 %reduce-scatter.11.cloned.1.call-start = ((), (), s32[]{:S(2)}) async-start(), calls=%async_computation.11 | async-start | bytes 294912 | tf_op jit(solution)/shard_map/reduce_scatter | solution.py:85
  511.1 4.3 collective-permute-start.21
  515.4 4.2 collective-permute-start.22
  528.1 4.2 collective-permute-start.25
  (8 other events, 176.2 us)
Sparse Core Ops, SparseCore 0:
  92.8 33.2 all-reduce.4
  138.2 33.7 reduce-scatter.4
  208.7 36.9 all-reduce.6
  251.2 33.4 reduce-scatter.6
  321.1 36.9 all-reduce.8
  363.6 33.4 reduce-scatter.8
  433.6 36.9 all-reduce.10
  476.8 33.4 reduce-scatter.10
